TPU v7x, 512 devices: a whole 4x8x8 slice. The times are simulated.
512 devices in a mesh: gx: 32 (over z, x), gy: 16 (over y, core).
Axes of the slice: x: 4, y: 8, z: 8, core: 2. Of those that a mesh axis runs over, the one named last changes fastest.
Arguments:
- source: float32 [2048, 256, 128], P('gx', 'gy'), may hold values from -5 to 5
Outputs:
- pressure: float32 [2048, 256, 128], P('gx', 'gy')
All inputs are finite; a program needn't handle non-finite values.
Results may differ from a plain program's by a relative error of at most 0.0003.
Values sent between devices are 32-bit elements; how exact they have to be, the bound alone decides.
A program may use at most 64 MiB of HBM per device.

v0:
```python
import math
import jax
import jax.numpy as jnp
from jax import lax
from jax.sharding import PartitionSpec as P

SCREEN = 32
highest = lax.Precision.HIGHEST


def cosine_table(points, wavenums, places):
    angles = wavenums[:, None] * (2 * places[None, :] + 1) % (4 * points)
    norming = jnp.where(wavenums == 0, math.sqrt(1.0 / points), math.sqrt(2.0 / points)).astype(
        jnp.float32
    )
    return norming[:, None] * jnp.cos(angles.astype(jnp.float32) * (math.pi / (2 * points)))


def eigenvalue(wavenums, points):
    half_angle = jnp.sin(wavenums.astype(jnp.float32) * (math.pi / (2 * points)))
    return 4.0 * half_angle * half_angle


def forward_cosine(received):
    length = received.shape[2]
    width = min(256, length)
    places = jnp.arange(length, dtype=jnp.int32)

    def forward_one_block(index, output):
        offset = index * width
        cos_table = cosine_table(length, offset + jnp.arange(width, dtype=jnp.int32), places)
        piece = jnp.einsum("zyx,kx->zyk", received, cos_table, precision=highest)
        return lax.dynamic_update_slice_in_dim(output, piece, offset, 2)

    return lax.fori_loop(
        0, length // width, forward_one_block, jnp.zeros(received.shape, jnp.float32)
    )


def backward_cosine(solved):
    length = solved.shape[2]
    width = min(256, length)
    waves = jnp.arange(length, dtype=jnp.int32)

    def backward_one_block(index, output):
        offset = index * width
        cos_table = cosine_table(length, waves, offset + jnp.arange(width, dtype=jnp.int32))
        piece = jnp.einsum("zyk,kx->zyx", solved, cos_table, precision=highest)
        return lax.dynamic_update_slice_in_dim(output, piece, offset, 2)

    return lax.fori_loop(
        0, length // width, backward_one_block, jnp.zeros(solved.shape, jnp.float32)
    )


def thomas(rhs_lines, diagonal):

    def forward_step(carry, source_line):
        factor, eliminated = carry
        factor = 1.0 / (diagonal - factor)
        eliminated = (source_line + eliminated) * factor
        return ((factor, eliminated), (factor, eliminated))

    empty_line = jnp.zeros_like(rhs_lines[0])
    unused, (factors, eliminated) = lax.scan(
        forward_step, (empty_line, empty_line), rhs_lines, unroll=8
    )

    def backward_step(pressure_next, inputs_line):
        solved_line = inputs_line[1] + inputs_line[0] * pressure_next
        return (solved_line, solved_line)

    unused_last, solution = lax.scan(
        backward_step, empty_line, (factors, eliminated), reverse=True, unroll=8
    )
    return solution


def shards(source):
    cx_cells, cy_cells, nz_cells = source.shape
    planes = nz_cells // lax.axis_size("gx")
    plane_first = lax.axis_index("gx") * planes
    nz_waves = jnp.arange(nz_cells, dtype=jnp.int32)
    z_table = cosine_table(nz_cells, nz_waves, nz_waves)
    zhat = jnp.einsum("xyz,kz->kyx", source, z_table, precision=highest)
    spectral = forward_cosine(lax.all_to_all(zhat, "gx", split_axis=0, concat_axis=2, tiled=True))
    nx_cells = spectral.shape[2]
    screen_shift = 1.0 / (SCREEN * SCREEN)
    z_eigen = eigenvalue(plane_first + jnp.arange(planes, dtype=jnp.int32), nz_cells)
    columns = lax.all_to_all(spectral, "gy", split_axis=2, concat_axis=1, tiled=True)
    column_count = columns.shape[2]
    column_first = lax.axis_index("gy") * column_count
    x_eigen = eigenvalue(column_first + jnp.arange(column_count, dtype=jnp.int32), nx_cells)
    diagonal = 2.0 + (screen_shift + z_eigen[:, None] + x_eigen[None, :])
    solved_columns = thomas(jnp.moveaxis(columns, 1, 0), diagonal)
    solved = lax.all_to_all(
        jnp.moveaxis(solved_columns, 0, 1), "gy", split_axis=1, concat_axis=2, tiled=True
    )
    physical = backward_cosine(solved)
    regrouped = lax.all_to_all(physical, "gx", split_axis=2, concat_axis=0, tiled=True)
    return jnp.einsum("kyx,kz->xyz", regrouped, z_table, precision=highest)


def solution(mesh):
    return jax.shard_map(
        shards,
        mesh=mesh,
        in_specs=(P("gx", "gy", None),),
        out_specs=P("gx", "gy", None),
        check_vma=False,
    )
```

profile of v0, /device:TPU:1, one launch (start us, length us, event | category | flops | bytes accessed | tf_op | source)
XLA Modules:
  0.0 354.0 jit_solution(14505402717037691400)
XLA Ops:
  3.9 13.7 %all-to-all-start = ((f32[32,1,4096]{2,1,0:T(1,128)}), f32[32,1,4096]{2,1,0:T(1,128)S(1)}, u32[]{:S(2)}, u32[]{:S(2)}) async-start(f32[32,1,4096]{2,1,0:T(1,128)} %reshape.126), calls=%async_computation | async-start | bytes 1048576 | tf_op jit(solution)/shard_map/all_to_all | solution.py:86
  17.6 16.3 %all-to-all-done = f32[32,1,4096]{2,1,0:T(1,128)S(1)} async-done(((f32[32,1,4096]{2,1,0:T(1,128)}), f32[32,1,4096]{2,1,0:T(1,128)S(1)}, u32[]{:S(2)}, u32[]{:S(2)}) %all-to-all-start) | async-done | bytes 524320 | tf_op jit(solution)/shard_map/all_to_all | solution.py:86
  37.8 77.5 %while.67 = (s32[]{:T(128)}, f32[4,16,2048]{2,1,0:T(8,128)S(1)}, f32[4,16,2048]{2,1,0:T(8,128)S(1)}, s32[]{:T(128)}, s32[]{:T(128)}, /*index=5*/s32[]{:T(128)}, s32[]{:T(128)}) while((s32[]{:T(128)}, f32[4,16,2048]{2,1,0:T(8,128)S(1)}, f32[4,16,2048]{2,1,0:T(8,128)S(1)}, s32[]{:T(128)}, s32[]{:T(128)}, /*index=5*/s32[]{:T(128)}, ...), condition=%wide.region_1.2_spmd.clone, body=%wide.region_0.1_spmd.clone.sunk | while | flops 410522624 | bytes 610439 | solution.py:35
  38.2 9.6 %fusion.161 = f32[4,16,2048]{2,1,0:T(8,128)S(1)} fusion(f32[4,16,2048]{2,1,0:T(8,128)S(1)} %get-tuple-element.753, s32[]{:T(128)S(6)} %select_n.174, f32[4,16,2048]{2,1,0:T(8,128)S(1)} %get-tuple-element.761, s32[2048]{0:T(1024)S(1)} %fusion.160, s32[256]{0:T(256)S(1)} %iota_add_fusion.2, f32[256]{0:T(256)S(1)} %compare_select_fusion.3), kind=kOutput, calls=%fused_computation.19.clone.1 | convolution fusion | flops 410517504 | bytes 600068 | tf_op jit(solution)/shard_map/while/body/eval_jaxpr/zyx,kx->zyk/dot_general | solution.py:32
  47.9 9.6 %fusion.161 = f32[4,16,2048]{2,1,0:T(8,128)S(1)} fusion(f32[4,16,2048]{2,1,0:T(8,128)S(1)} %get-tuple-element.753, s32[]{:T(128)S(6)} %select_n.174, f32[4,16,2048]{2,1,0:T(8,128)S(1)} %get-tuple-element.761, s32[2048]{0:T(1024)S(1)} %fusion.160, s32[256]{0:T(256)S(1)} %iota_add_fusion.2, f32[256]{0:T(256)S(1)} %compare_select_fusion.3), kind=kOutput, calls=%fused_computation.19.clone.1 | convolution fusion | flops 410517504 | bytes 600068 | tf_op jit(solution)/shard_map/while/body/eval_jaxpr/zyx,kx->zyk/dot_general | solution.py:32
  57.5 9.6 %fusion.161 = f32[4,16,2048]{2,1,0:T(8,128)S(1)} fusion(f32[4,16,2048]{2,1,0:T(8,128)S(1)} %get-tuple-element.753, s32[]{:T(128)S(6)} %select_n.174, f32[4,16,2048]{2,1,0:T(8,128)S(1)} %get-tuple-element.761, s32[2048]{0:T(1024)S(1)} %fusion.160, s32[256]{0:T(256)S(1)} %iota_add_fusion.2, f32[256]{0:T(256)S(1)} %compare_select_fusion.3), kind=kOutput, calls=%fused_computation.19.clone.1 | convolution fusion | flops 410517504 | bytes 600068 | tf_op jit(solution)/shard_map/while/body/eval_jaxpr/zyx,kx->zyk/dot_general | solution.py:32
  67.2 9.6 %fusion.161 = f32[4,16,2048]{2,1,0:T(8,128)S(1)} fusion(f32[4,16,2048]{2,1,0:T(8,128)S(1)} %get-tuple-element.753, s32[]{:T(128)S(6)} %select_n.174, f32[4,16,2048]{2,1,0:T(8,128)S(1)} %get-tuple-element.761, s32[2048]{0:T(1024)S(1)} %fusion.160, s32[256]{0:T(256)S(1)} %iota_add_fusion.2, f32[256]{0:T(256)S(1)} %compare_select_fusion.3), kind=kOutput, calls=%fused_computation.19.clone.1 | convolution fusion | flops 410517504 | bytes 600068 | tf_op jit(solution)/shard_map/while/body/eval_jaxpr/zyx,kx->zyk/dot_general | solution.py:32
  76.8 9.6 %fusion.161 = f32[4,16,2048]{2,1,0:T(8,128)S(1)} fusion(f32[4,16,2048]{2,1,0:T(8,128)S(1)} %get-tuple-element.753, s32[]{:T(128)S(6)} %select_n.174, f32[4,16,2048]{2,1,0:T(8,128)S(1)} %get-tuple-element.761, s32[2048]{0:T(1024)S(1)} %fusion.160, s32[256]{0:T(256)S(1)} %iota_add_fusion.2, f32[256]{0:T(256)S(1)} %compare_select_fusion.3), kind=kOutput, calls=%fused_computation.19.clone.1 | convolution fusion | flops 410517504 | bytes 600068 | tf_op jit(solution)/shard_map/while/body/eval_jaxpr/zyx,kx->zyk/dot_general | solution.py:32
  86.5 9.6 %fusion.161 = f32[4,16,2048]{2,1,0:T(8,128)S(1)} fusion(f32[4,16,2048]{2,1,0:T(8,128)S(1)} %get-tuple-element.753, s32[]{:T(128)S(6)} %select_n.174, f32[4,16,2048]{2,1,0:T(8,128)S(1)} %get-tuple-element.761, s32[2048]{0:T(1024)S(1)} %fusion.160, s32[256]{0:T(256)S(1)} %iota_add_fusion.2, f32[256]{0:T(256)S(1)} %compare_select_fusion.3), kind=kOutput, calls=%fused_computation.19.clone.1 | convolution fusion | flops 410517504 | bytes 600068 | tf_op jit(solution)/shard_map/while/body/eval_jaxpr/zyx,kx->zyk/dot_general | solution.py:32
  96.1 9.6 %fusion.161 = f32[4,16,2048]{2,1,0:T(8,128)S(1)} fusion(f32[4,16,2048]{2,1,0:T(8,128)S(1)} %get-tuple-element.753, s32[]{:T(128)S(6)} %select_n.174, f32[4,16,2048]{2,1,0:T(8,128)S(1)} %get-tuple-element.761, s32[2048]{0:T(1024)S(1)} %fusion.160, s32[256]{0:T(256)S(1)} %iota_add_fusion.2, f32[256]{0:T(256)S(1)} %compare_select_fusion.3), kind=kOutput, calls=%fused_computation.19.clone.1 | convolution fusion | flops 410517504 | bytes 600068 | tf_op jit(solution)/shard_map/while/body/eval_jaxpr/zyx,kx->zyk/dot_general | solution.py:32
  105.7 9.6 %fusion.161 = f32[4,16,2048]{2,1,0:T(8,128)S(1)} fusion(f32[4,16,2048]{2,1,0:T(8,128)S(1)} %get-tuple-element.753, s32[]{:T(128)S(6)} %select_n.174, f32[4,16,2048]{2,1,0:T(8,128)S(1)} %get-tuple-element.761, s32[2048]{0:T(1024)S(1)} %fusion.160, s32[256]{0:T(256)S(1)} %iota_add_fusion.2, f32[256]{0:T(256)S(1)} %compare_select_fusion.3), kind=kOutput, calls=%fused_computation.19.clone.1 | convolution fusion | flops 410517504 | bytes 600068 | tf_op jit(solution)/shard_map/while/body/eval_jaxpr/zyx,kx->zyk/dot_general | solution.py:32
  118.4 5.4 %reshape.128 = f32[16,1,8192]{2,1,0:T(1,128)} reshape(f32[2048,4,16]{2,1,0:T(4,128)} %bitcast.312) | data formatting | bytes 1048576
  123.8 9.5 %all-to-all-start.1 = ((f32[16,1,8192]{2,1,0:T(1,128)}), f32[16,1,8192]{2,1,0:T(1,128)S(1)}, u32[]{:S(2)}, u32[]{:S(2)}) async-start(f32[16,1,8192]{2,1,0:T(1,128)} %reshape.128), calls=%async_computation.1 | async-start | bytes 1048576 | tf_op jit(solution)/shard_map/all_to_all | solution.py:90
  133.5 17.2 %all-to-all-done.1 = f32[16,1,8192]{2,1,0:T(1,128)S(1)} async-done(((f32[16,1,8192]{2,1,0:T(1,128)}), f32[16,1,8192]{2,1,0:T(1,128)S(1)}, u32[]{:S(2)}, u32[]{:S(2)}) %all-to-all-start.1) | async-done | bytes 524320 | tf_op jit(solution)/shard_map/all_to_all | solution.py:90
  152.6 4.3 %reshape.129 = f32[2048,4,16]{2,1,0:T(4,128)} reshape(f32[16,8192]{1,0:T(8,128)S(1)} %reduce.1) | data formatting | bytes 1048576
  160.5 26.0 %while.69 = (s32[]{:T(128)}, f32[4,128]{1,0:T(4,128)S(1)}, f32[4,128]{1,0:T(4,128)S(1)}, f32[32,8,4,128]{3,2,1,0:T(4,128)S(1)}, f32[32,8,4,128]{3,2,1,0:T(4,128)...) while((s32[]{:T(128)}, f32[4,128]{1,0:T(4,128)S(1)}, ...), condition=%wide.region_3.4_spmd.clone, body=%wide.region_2.3_spmd.clone.sunk | while | flops 33288 | bytes 220976 | solution.py:65
  187.5 23.0 %while.70 = (s32[]{:T(128)}, f32[4,128]{1,0:T(4,128)S(1)}, f32[32,8,4,128]{3,2,1,0:T(4,128)}, f32[32,8,4,128]{3,2,1,0:T(4,128)S(1)}, f32[32,8,4,128]{3,2,1,0:T(4...) while((s32[]{:T(128)}, f32[4,128]{1,0:T(4,128)S(1)}, ...), condition=%wide.region_5.6_spmd.clone, body=%wide.region_4.5_spmd.clone.sunk | while | flops 8714 | bytes 114971 | solution.py:73
  210.5 12.1 %all-to-all-start.2 = ((f32[4,256,128]{2,0,1:T(4,128)}), f32[4,256,128]{2,0,1:T(4,128)S(1)}, u32[]{:S(2)}, u32[]{:S(2)}) async-start(f32[4,256,128]{2,0,1:T(4,128)} %bitcast.11), calls=%async_computation.2 | async-start | bytes 1048576 | tf_op jit(solution)/shard_map/all_to_all | solution.py:96
  222.6 16.5 %all-to-all-done.2 = f32[4,256,128]{2,0,1:T(4,128)S(1)} async-done(((f32[4,256,128]{2,0,1:T(4,128)}), f32[4,256,128]{2,0,1:T(4,128)S(1)}, u32[]{:S(2)}, u32[]{:S(2)}) %all-to-all-start.2) | async-done | bytes 524320 | tf_op jit(solution)/shard_map/all_to_all | solution.py:96
  239.6 73.0 %while.68 = (s32[]{:T(128)}, f32[4,16,2048]{2,1,0:T(8,128)S(1)}, f32[4,16,2048]{2,1,0:T(8,128)S(1)}, s32[]{:T(128)}, s32[]{:T(128)}, /*index=5*/s32[]{:T(128)}, s32[]{:T(128)}) while((s32[]{:T(128)}, f32[4,16,2048]{2,1,0:T(8,128)S(1)}, f32[4,16,2048]{2,1,0:T(8,128)S(1)}, s32[]{:T(128)}, s32[]{:T(128)}, ...), condition=%wide.region_7.8_spmd.clone.clone, body=%wide.region_6.7_spmd.clone.clone.sunk | while | flops 410522368 | bytes 608387 | solution.py:51
  239.6 9.1 %fusion.165 = f32[4,16,2048]{2,1,0:T(8,128)S(1)} fusion(f32[4,16,2048]{2,1,0:T(8,128)S(1)} %get-tuple-element.870, s32[]{:T(128)S(6)} %select_n.177, f32[4,16,2048]{2,1,0:T(8,128)S(1)} %get-tuple-element.878, s32[256]{0:T(256)S(1)} %multiply_add_fusion.3, f32[2048]{0:T(1024)S(1)} %fusion.164), kind=kOutput, calls=%fused_computation.50.clone.1 | convolution fusion | flops 410517504 | bytes 599044 | tf_op jit(solution)/shard_map/while/body/eval_jaxpr/zyk,kx->zyx/dot_general | solution.py:48
  248.7 9.1 %fusion.165 = f32[4,16,2048]{2,1,0:T(8,128)S(1)} fusion(f32[4,16,2048]{2,1,0:T(8,128)S(1)} %get-tuple-element.870, s32[]{:T(128)S(6)} %select_n.177, f32[4,16,2048]{2,1,0:T(8,128)S(1)} %get-tuple-element.878, s32[256]{0:T(256)S(1)} %multiply_add_fusion.3, f32[2048]{0:T(1024)S(1)} %fusion.164), kind=kOutput, calls=%fused_computation.50.clone.1 | convolution fusion | flops 410517504 | bytes 599044 | tf_op jit(solution)/shard_map/while/body/eval_jaxpr/zyk,kx->zyx/dot_general | solution.py:48
  257.9 9.1 %fusion.165 = f32[4,16,2048]{2,1,0:T(8,128)S(1)} fusion(f32[4,16,2048]{2,1,0:T(8,128)S(1)} %get-tuple-element.870, s32[]{:T(128)S(6)} %select_n.177, f32[4,16,2048]{2,1,0:T(8,128)S(1)} %get-tuple-element.878, s32[256]{0:T(256)S(1)} %multiply_add_fusion.3, f32[2048]{0:T(1024)S(1)} %fusion.164), kind=kOutput, calls=%fused_computation.50.clone.1 | convolution fusion | flops 410517504 | bytes 599044 | tf_op jit(solution)/shard_map/while/body/eval_jaxpr/zyk,kx->zyx/dot_general | solution.py:48
  267.0 9.1 %fusion.165 = f32[4,16,2048]{2,1,0:T(8,128)S(1)} fusion(f32[4,16,2048]{2,1,0:T(8,128)S(1)} %get-tuple-element.870, s32[]{:T(128)S(6)} %select_n.177, f32[4,16,2048]{2,1,0:T(8,128)S(1)} %get-tuple-element.878, s32[256]{0:T(256)S(1)} %multiply_add_fusion.3, f32[2048]{0:T(1024)S(1)} %fusion.164), kind=kOutput, calls=%fused_computation.50.clone.1 | convolution fusion | flops 410517504 | bytes 599044 | tf_op jit(solution)/shard_map/while/body/eval_jaxpr/zyk,kx->zyx/dot_general | solution.py:48
  276.1 9.1 %fusion.165 = f32[4,16,2048]{2,1,0:T(8,128)S(1)} fusion(f32[4,16,2048]{2,1,0:T(8,128)S(1)} %get-tuple-element.870, s32[]{:T(128)S(6)} %select_n.177, f32[4,16,2048]{2,1,0:T(8,128)S(1)} %get-tuple-element.878, s32[256]{0:T(256)S(1)} %multiply_add_fusion.3, f32[2048]{0:T(1024)S(1)} %fusion.164), kind=kOutput, calls=%fused_computation.50.clone.1 | convolution fusion | flops 410517504 | bytes 599044 | tf_op jit(solution)/shard_map/while/body/eval_jaxpr/zyk,kx->zyx/dot_general | solution.py:48
  285.2 9.1 %fusion.165 = f32[4,16,2048]{2,1,0:T(8,128)S(1)} fusion(f32[4,16,2048]{2,1,0:T(8,128)S(1)} %get-tuple-element.870, s32[]{:T(128)S(6)} %select_n.177, f32[4,16,2048]{2,1,0:T(8,128)S(1)} %get-tuple-element.878, s32[256]{0:T(256)S(1)} %multiply_add_fusion.3, f32[2048]{0:T(1024)S(1)} %fusion.164), kind=kOutput, calls=%fused_computation.50.clone.1 | convolution fusion | flops 410517504 | bytes 599044 | tf_op jit(solution)/shard_map/while/body/eval_jaxpr/zyk,kx->zyx/dot_general | solution.py:48
  294.4 9.1 %fusion.165 = f32[4,16,2048]{2,1,0:T(8,128)S(1)} fusion(f32[4,16,2048]{2,1,0:T(8,128)S(1)} %get-tuple-element.870, s32[]{:T(128)S(6)} %select_n.177, f32[4,16,2048]{2,1,0:T(8,128)S(1)} %get-tuple-element.878, s32[256]{0:T(256)S(1)} %multiply_add_fusion.3, f32[2048]{0:T(1024)S(1)} %fusion.164), kind=kOutput, calls=%fused_computation.50.clone.1 | convolution fusion | flops 410517504 | bytes 599044 | tf_op jit(solution)/shard_map/while/body/eval_jaxpr/zyk,kx->zyx/dot_general | solution.py:48
  303.5 9.1 %fusion.165 = f32[4,16,2048]{2,1,0:T(8,128)S(1)} fusion(f32[4,16,2048]{2,1,0:T(8,128)S(1)} %get-tuple-element.870, s32[]{:T(128)S(6)} %select_n.177, f32[4,16,2048]{2,1,0:T(8,128)S(1)} %get-tuple-element.878, s32[256]{0:T(256)S(1)} %multiply_add_fusion.3, f32[2048]{0:T(1024)S(1)} %fusion.164), kind=kOutput, calls=%fused_computation.50.clone.1 | convolution fusion | flops 410517504 | bytes 599044 | tf_op jit(solution)/shard_map/while/body/eval_jaxpr/zyk,kx->zyx/dot_general | solution.py:48
  315.6 4.8 %reshape.130 = f32[32,1,4096]{2,1,0:T(1,128)S(1)} reshape(f32[2048,4,16]{2,1,0:T(4,128)} %bitcast.314) | data formatting | bytes 1048576
  320.4 21.3 %all_to_all.72 = f32[32,1,4096]{2,1,0:T(1,128)S(1)} all-to-all(f32[32,1,4096]{2,1,0:T(1,128)S(1)} %reshape.130), channel_id=1, replica_groups=mesh['gx'=32,'gy'=16] {'gx'}, dimensions={0} | all-to-all | bytes 1048576 | tf_op jit(solution)/shard_map/all_to_all | solution.py:100
  343.7 4.3 %reshape.131 = f32[2048,4,16]{2,1,0:T(4,128)} reshape(f32[32,4096]{1,0:T(8,128)S(1)} %reduce.2) | data formatting | bytes 1048576
  347.9 3.5 copy.51
  (808 shorter events, 71.9 us)
Async XLA Ops:
  0.0 1.0 copy-start
  3.9 30.0 %all-to-all-start = ((f32[32,1,4096]{2,1,0:T(1,128)}), f32[32,1,4096]{2,1,0:T(1,128)S(1)}, u32[]{:S(2)}, u32[]{:S(2)}) async-start(f32[32,1,4096]{2,1,0:T(1,128)} %reshape.126), calls=%async_computation | async-start | bytes 1048576 | tf_op jit(solution)/shard_map/all_to_all | solution.py:86
  123.8 26.8 %all-to-all-start.1 = ((f32[16,1,8192]{2,1,0:T(1,128)}), f32[16,1,8192]{2,1,0:T(1,128)S(1)}, u32[]{:S(2)}, u32[]{:S(2)}) async-start(f32[16,1,8192]{2,1,0:T(1,128)} %reshape.128), calls=%async_computation.1 | async-start | bytes 1048576 | tf_op jit(solution)/shard_map/all_to_all | solution.py:90
  210.5 28.6 %all-to-all-start.2 = ((f32[4,256,128]{2,0,1:T(4,128)}), f32[4,256,128]{2,0,1:T(4,128)S(1)}, u32[]{:S(2)}, u32[]{:S(2)}) async-start(f32[4,256,128]{2,0,1:T(4,128)} %bitcast.11), calls=%async_computation.2 | async-start | bytes 1048576 | tf_op jit(solution)/shard_map/all_to_all | solution.py:96
where the time goes:
time: 359 us; the launch traced here: 354 us
  matrix products  151 us (42%)
  local copies, waits for them, and re-layouts  64.1 us (18%)
  waiting for transfers between devices  50 us (14%)
  starting transfers between devices  35.4 us (10%)
  other arithmetic  28.3 us (8%)
  blocking collectives  21.3 us (6%)
    dot_general x8, matrix products, forward_one_block(): piece = jnp.einsum('zyx,kx->zyk', received, cos_table, precision=highest)  76.7 us
    dot_general x8, matrix products, backward_one_block(): piece = jnp.einsum('zyk,kx->zyx', solved, cos_table, precision=highest)  72.7 us
    unnamed x8, local copies, waits for them, and re-layouts  21.6 us
    all_to_all x1, blocking collectives, shards(): lax.all_to_all(physical, 'gx', split_axis=2, concat_axis=0, tiled=True)  21.3 us
    dynamic_update_slice x64, local copies, waits for them, and re-layouts, thomas(): lax.scan(forward_step, (empty_line, empty_line), rhs_lines, unroll=8)  20.1 us
    while x256, other arithmetic  19.5 us
    all_to_all x1, waiting for transfers between devices, shards(): lax.all_to_all(spectral, 'gy', split_axis=2, concat_axis=1, tiled=True)  17.2 us
    all_to_all x1, waiting for transfers between devices, shards(): lax.all_to_all(jnp.moveaxis(solved_columns, 0, 1), 'gy', split_axis=1, co...  16.5 us
  transfers between devices with their start and end apart: 3, of which 3 were waited for; matrix products, arithmetic and copies ran while one was open for 0% of the time, Pallas kernels for 0%

commit v1 on v0

--- a/solution.py
+++ b/solution.py
@@ -3,9 +3,32 @@
 import jax.numpy as jnp
 from jax import lax
 from jax.sharding import PartitionSpec as P
+from jax.lax import axis_index, ppermute, psum
 
 SCREEN = 32
 highest = lax.Precision.HIGHEST
+
+
+def arrange_column(block_in, peer_axis="gy"):
+    upper = psum(1, peer_axis)
+    arr_now = axis_index(peer_axis)
+    small, aux = (upper, arr_now)
+    base_arr = list(block_in.shape)
+    block_out = block_in.shape[1] // small
+    base_arr[1] = block_out
+    built = base_arr[2]
+    base_arr[2] = built * small
+    state_next = jnp.zeros(base_arr, block_in.dtype)
+    tick = 0
+    while tick < small:
+        x_now = lax.dynamic_slice_in_dim(block_in, (aux ^ tick) * block_out, block_out, axis=1)
+        if tick:
+            x_now = ppermute(x_now, peer_axis, [(m, m ^ tick) for m in range(small)])
+        state_next = lax.dynamic_update_slice_in_dim(
+            state_next, x_now, (aux ^ tick) * built, axis=2
+        )
+        tick += 1
+    return state_next
 
 
 def cosine_table(points, wavenums, places):
@@ -93,9 +116,7 @@
     x_eigen = eigenvalue(column_first + jnp.arange(column_count, dtype=jnp.int32), nx_cells)
     diagonal = 2.0 + (screen_shift + z_eigen[:, None] + x_eigen[None, :])
     solved_columns = thomas(jnp.moveaxis(columns, 1, 0), diagonal)
-    solved = lax.all_to_all(
-        jnp.moveaxis(solved_columns, 0, 1), "gy", split_axis=1, concat_axis=2, tiled=True
-    )
+    solved = arrange_column(jnp.moveaxis(solved_columns, 0, 1))
     physical = backward_cosine(solved)
     regrouped = lax.all_to_all(physical, "gx", split_axis=2, concat_axis=0, tiled=True)
     return jnp.einsum("kyx,kz->xyz", regrouped, z_table, precision=highest)

time: 359 us -> 382 us (1.064)
  starting transfers between devices: 35.4 us -> 89 us
  local copies, waits for them, and re-layouts: 64.1 us -> 44.2 us
  waiting for transfers between devices: 50 us -> 34.6 us
    ppermute x0 -> x15, starting transfers between devices: none -> 54.2 us  [arrange_column(): x_now = ppermute(x_now, peer_axis, [(m, m ^ tick) for m in range(small)])]
    dynamic_update_slice x64, local copies, waits for them, and re-layouts: 20.1 us -> 0.99 us  [thomas(): lax.scan(forward_step, (empty_line, empty_line), rhs_lines, unroll=8)]
    all_to_all x1 -> x0, waiting for transfers between devices: 16.5 us -> none  [shards(): lax.all_to_all(jnp.moveaxis(solved_columns, 0, 1), 'gy', split_axis=1, co...]
    all_to_all x1 -> x0, starting transfers between devices: 12.1 us -> none  [shards(): lax.all_to_all(jnp.moveaxis(solved_columns, 0, 1), 'gy', split_axis=1, co...]
    all_to_all x1, starting transfers between devices: 9.5 us -> 21.1 us  [shards(): lax.all_to_all(spectral, 'gy', split_axis=2, concat_axis=1, tiled=True)]
    unnamed x8 -> x23, local copies, waits for them, and re-layouts: 21.6 us -> 21.7 us
  transfers between devices with their start and end apart: 3 -> 17, of which waited for: 3 -> 3; matrix products, arithmetic and copies ran while one was open for 0% -> 0% of each run, Pallas kernels for 0% -> 0%
where the time goes in v1:
time: 382 us; the launch traced here: 374 us
  matrix products  151 us (40%)
  starting transfers between devices  89 us (23%)
  local copies, waits for them, and re-layouts  44.2 us (12%)
  waiting for transfers between devices  34.6 us (9%)
  other arithmetic  29 us (8%)
  blocking collectives  21 us (5%)
  loops' own time  4.22 us (1%)
    dot_general x8, matrix products, forward_one_block(): piece = jnp.einsum('zyx,kx->zyk', received, cos_table, precision=highest)  76.7 us
    dot_general x8, matrix products, backward_one_block(): piece = jnp.einsum('zyk,kx->zyx', solved, cos_table, precision=highest)  72.6 us
    ppermute x15, starting transfers between devices, arrange_column(): x_now = ppermute(x_now, peer_axis, [(m, m ^ tick) for m in range(small)])  54.2 us
    unnamed x23, local copies, waits for them, and re-layouts  21.7 us
    all_to_all x1, starting transfers between devices, shards(): lax.all_to_all(spectral, 'gy', split_axis=2, concat_axis=1, tiled=True)  21.1 us
    all_to_all x1, blocking collectives, shards(): lax.all_to_all(physical, 'gx', split_axis=2, concat_axis=0, tiled=True)  21 us
    while x256, other arithmetic  20.3 us
    all_to_all x1, waiting for transfers between devices, shards(): lax.all_to_all(spectral, 'gy', split_axis=2, concat_axis=1, tiled=True)  16.8 us
  transfers between devices with their start and end apart: 17, of which 3 were waited for; matrix products, arithmetic and copies ran while one was open for 0% of the time, Pallas kernels for 0%

profile of v1, /device:TPU:1, one launch (start us, length us, event | category | flops | bytes accessed | tf_op | source)
XLA Modules:
  0.0 374.2 jit_solution(8184484392525721907)
XLA Ops:
  3.9 13.7 %all-to-all-start = ((f32[32,1,4096]{2,1,0:T(1,128)}), f32[32,1,4096]{2,1,0:T(1,128)S(1)}, u32[]{:S(2)}, u32[]{:S(2)}) async-start(f32[32,1,4096]{2,1,0:T(1,128)} %reshape.126), calls=%async_computation | async-start | bytes 1048576 | tf_op jit(solution)/shard_map/all_to_all | solution.py:109
  17.6 16.3 %all-to-all-done = f32[32,1,4096]{2,1,0:T(1,128)S(1)} async-done(((f32[32,1,4096]{2,1,0:T(1,128)}), f32[32,1,4096]{2,1,0:T(1,128)S(1)}, u32[]{:S(2)}, u32[]{:S(2)}) %all-to-all-start) | async-done | bytes 524320 | tf_op jit(solution)/shard_map/all_to_all | solution.py:109
  37.8 77.5 %while.67 = (s32[]{:T(128)}, f32[4,16,2048]{2,1,0:T(8,128)S(1)}, f32[4,16,2048]{2,1,0:T(8,128)S(1)}, s32[]{:T(128)}, s32[]{:T(128)}, /*index=5*/s32[]{:T(128)}, s32[]{:T(128)}) while((s32[]{:T(128)}, f32[4,16,2048]{2,1,0:T(8,128)S(1)}, f32[4,16,2048]{2,1,0:T(8,128)S(1)}, s32[]{:T(128)}, s32[]{:T(128)}, /*index=5*/s32[]{:T(128)}, ...), condition=%wide.region_1.2_spmd.clone, body=%wide.region_0.1_spmd.clone.sunk | while | flops 410522624 | bytes 610439 | solution.py:58
  38.2 9.6 %fusion.162 = f32[4,16,2048]{2,1,0:T(8,128)S(1)} fusion(f32[4,16,2048]{2,1,0:T(8,128)S(1)} %get-tuple-element.769, s32[]{:T(128)S(6)} %select_n.302, f32[4,16,2048]{2,1,0:T(8,128)S(1)} %get-tuple-element.777, s32[2048]{0:T(1024)S(1)} %fusion.161, s32[256]{0:T(256)S(1)} %iota_add_fusion.2, f32[256]{0:T(256)S(1)} %compare_select_fusion.3), kind=kOutput, calls=%fused_computation.19.clone.1 | convolution fusion | flops 410517504 | bytes 600068 | tf_op jit(solution)/shard_map/while/body/eval_jaxpr/zyx,kx->zyk/dot_general | solution.py:55
  47.8 9.6 %fusion.162 = f32[4,16,2048]{2,1,0:T(8,128)S(1)} fusion(f32[4,16,2048]{2,1,0:T(8,128)S(1)} %get-tuple-element.769, s32[]{:T(128)S(6)} %select_n.302, f32[4,16,2048]{2,1,0:T(8,128)S(1)} %get-tuple-element.777, s32[2048]{0:T(1024)S(1)} %fusion.161, s32[256]{0:T(256)S(1)} %iota_add_fusion.2, f32[256]{0:T(256)S(1)} %compare_select_fusion.3), kind=kOutput, calls=%fused_computation.19.clone.1 | convolution fusion | flops 410517504 | bytes 600068 | tf_op jit(solution)/shard_map/while/body/eval_jaxpr/zyx,kx->zyk/dot_general | solution.py:55
  57.5 9.6 %fusion.162 = f32[4,16,2048]{2,1,0:T(8,128)S(1)} fusion(f32[4,16,2048]{2,1,0:T(8,128)S(1)} %get-tuple-element.769, s32[]{:T(128)S(6)} %select_n.302, f32[4,16,2048]{2,1,0:T(8,128)S(1)} %get-tuple-element.777, s32[2048]{0:T(1024)S(1)} %fusion.161, s32[256]{0:T(256)S(1)} %iota_add_fusion.2, f32[256]{0:T(256)S(1)} %compare_select_fusion.3), kind=kOutput, calls=%fused_computation.19.clone.1 | convolution fusion | flops 410517504 | bytes 600068 | tf_op jit(solution)/shard_map/while/body/eval_jaxpr/zyx,kx->zyk/dot_general | solution.py:55
  67.1 9.6 %fusion.162 = f32[4,16,2048]{2,1,0:T(8,128)S(1)} fusion(f32[4,16,2048]{2,1,0:T(8,128)S(1)} %get-tuple-element.769, s32[]{:T(128)S(6)} %select_n.302, f32[4,16,2048]{2,1,0:T(8,128)S(1)} %get-tuple-element.777, s32[2048]{0:T(1024)S(1)} %fusion.161, s32[256]{0:T(256)S(1)} %iota_add_fusion.2, f32[256]{0:T(256)S(1)} %compare_select_fusion.3), kind=kOutput, calls=%fused_computation.19.clone.1 | convolution fusion | flops 410517504 | bytes 600068 | tf_op jit(solution)/shard_map/while/body/eval_jaxpr/zyx,kx->zyk/dot_general | solution.py:55
  76.8 9.6 %fusion.162 = f32[4,16,2048]{2,1,0:T(8,128)S(1)} fusion(f32[4,16,2048]{2,1,0:T(8,128)S(1)} %get-tuple-element.769, s32[]{:T(128)S(6)} %select_n.302, f32[4,16,2048]{2,1,0:T(8,128)S(1)} %get-tuple-element.777, s32[2048]{0:T(1024)S(1)} %fusion.161, s32[256]{0:T(256)S(1)} %iota_add_fusion.2, f32[256]{0:T(256)S(1)} %compare_select_fusion.3), kind=kOutput, calls=%fused_computation.19.clone.1 | convolution fusion | flops 410517504 | bytes 600068 | tf_op jit(solution)/shard_map/while/body/eval_jaxpr/zyx,kx->zyk/dot_general | solution.py:55
  86.4 9.6 %fusion.162 = f32[4,16,2048]{2,1,0:T(8,128)S(1)} fusion(f32[4,16,2048]{2,1,0:T(8,128)S(1)} %get-tuple-element.769, s32[]{:T(128)S(6)} %select_n.302, f32[4,16,2048]{2,1,0:T(8,128)S(1)} %get-tuple-element.777, s32[2048]{0:T(1024)S(1)} %fusion.161, s32[256]{0:T(256)S(1)} %iota_add_fusion.2, f32[256]{0:T(256)S(1)} %compare_select_fusion.3), kind=kOutput, calls=%fused_computation.19.clone.1 | convolution fusion | flops 410517504 | bytes 600068 | tf_op jit(solution)/shard_map/while/body/eval_jaxpr/zyx,kx->zyk/dot_general | solution.py:55
  96.1 9.6 %fusion.162 = f32[4,16,2048]{2,1,0:T(8,128)S(1)} fusion(f32[4,16,2048]{2,1,0:T(8,128)S(1)} %get-tuple-element.769, s32[]{:T(128)S(6)} %select_n.302, f32[4,16,2048]{2,1,0:T(8,128)S(1)} %get-tuple-element.777, s32[2048]{0:T(1024)S(1)} %fusion.161, s32[256]{0:T(256)S(1)} %iota_add_fusion.2, f32[256]{0:T(256)S(1)} %compare_select_fusion.3), kind=kOutput, calls=%fused_computation.19.clone.1 | convolution fusion | flops 410517504 | bytes 600068 | tf_op jit(solution)/shard_map/while/body/eval_jaxpr/zyx,kx->zyk/dot_general | solution.py:55
  105.7 9.6 %fusion.162 = f32[4,16,2048]{2,1,0:T(8,128)S(1)} fusion(f32[4,16,2048]{2,1,0:T(8,128)S(1)} %get-tuple-element.769, s32[]{:T(128)S(6)} %select_n.302, f32[4,16,2048]{2,1,0:T(8,128)S(1)} %get-tuple-element.777, s32[2048]{0:T(1024)S(1)} %fusion.161, s32[256]{0:T(256)S(1)} %iota_add_fusion.2, f32[256]{0:T(256)S(1)} %compare_select_fusion.3), kind=kOutput, calls=%fused_computation.19.clone.1 | convolution fusion | flops 410517504 | bytes 600068 | tf_op jit(solution)/shard_map/while/body/eval_jaxpr/zyx,kx->zyk/dot_general | solution.py:55
  118.3 5.4 %reshape.128 = f32[16,1,8192]{2,1,0:T(1,128)} reshape(f32[2048,4,16]{2,1,0:T(4,128)} %bitcast.353) | data formatting | bytes 1048576
  123.8 21.1 %all-to-all-start.1 = ((f32[16,1,8192]{2,1,0:T(1,128)}), f32[16,1,8192]{2,1,0:T(1,128)S(1)}, u32[]{:S(2)}, u32[]{:S(2)}) async-start(f32[16,1,8192]{2,1,0:T(1,128)} %reshape.128), calls=%async_computation.1 | async-start | bytes 1048576 | tf_op jit(solution)/shard_map/all_to_all | solution.py:113
  145.3 16.8 %all-to-all-done.1 = f32[16,1,8192]{2,1,0:T(1,128)S(1)} async-done(((f32[16,1,8192]{2,1,0:T(1,128)}), f32[16,1,8192]{2,1,0:T(1,128)S(1)}, u32[]{:S(2)}, u32[]{:S(2)}) %all-to-all-start.1) | async-done | bytes 524320 | tf_op jit(solution)/shard_map/all_to_all | solution.py:113
  171.9 26.0 %while.69 = (s32[]{:T(128)}, f32[4,128]{1,0:T(4,128)S(1)}, f32[4,128]{1,0:T(4,128)S(1)}, f32[32,8,4,128]{3,2,1,0:T(4,128)S(1)}, f32[32,8,4,128]{3,2,1,0:T(4,128)...) while((s32[]{:T(128)}, f32[4,128]{1,0:T(4,128)S(1)}, ...), condition=%wide.region_3.4_spmd.clone, body=%wide.region_2.3_spmd.clone.sunk | while | flops 33288 | bytes 220976 | solution.py:88
  198.0 5.5 %while.70 = (s32[]{:T(128)}, f32[4,128]{1,0:T(4,128)S(1)}, f32[32,8,4,128]{3,2,1,0:T(4,128)S(1)}, f32[32,8,4,128]{3,2,1,0:T(4,128)S(1)}, f32[32,8,4,128]{3,2,1,0...) while((s32[]{:T(128)}, f32[4,128]{1,0:T(4,128)S(1)}, ...), condition=%wide.region_5.6_spmd.clone, body=%wide.region_4.5_spmd.clone.sunk | while | flops 8714 | bytes 114971 | solution.py:96
  221.1 4.5 %collective-permute-start.6 = (f32[4,16,128]{2,1,0:T(8,128)S(1)}, f32[4,16,128]{2,1,0:T(8,128)S(1)}, u32[]{:S(2)}, u32[]{:S(2)}) collective-permute-start(f32[4,16,128]{2,1,0:T(8,128)S(1)} %bitcast.381), channel_id=1, source_target_pairs={{0,7},{1,6},{2,5},{3,4},{4,3},{5,2},{6,1},{7,0},{8,15},{9,14},{10,... | collective-permute-start | bytes 98312 | tf_op jit(solution)/shard_map/ppermute | solution.py:26
  228.7 6.2 %collective-permute-start.8 = (f32[4,16,128]{2,1,0:T(8,128)S(1)}, f32[4,16,128]{2,1,0:T(8,128)S(1)}, u32[]{:S(2)}, u32[]{:S(2)}) collective-permute-start(f32[4,16,128]{2,1,0:T(8,128)S(1)} %bitcast.379), channel_id=1, source_target_pairs={{0,9},{1,8},{2,11},{3,10},{4,13},{5,12},{6,15},{7,14},{8,1},{9,0},... | collective-permute-start | bytes 98312 | tf_op jit(solution)/shard_map/ppermute | solution.py:26
  236.8 7.0 %collective-permute-start.10 = (f32[4,16,128]{2,1,0:T(8,128)S(1)}, f32[4,16,128]{2,1,0:T(8,128)S(1)}, u32[]{:S(2)}, u32[]{:S(2)}) collective-permute-start(f32[4,16,128]{2,1,0:T(8,128)S(1)} %bitcast.377), channel_id=1, source_target_pairs={{0,11},{1,10},{2,9},{3,8},{4,15},{5,14},{6,13},{7,12},{8,3},{9,2},... | collective-permute-start | bytes 98312 | tf_op jit(solution)/shard_map/ppermute | solution.py:26
  245.9 5.4 %collective-permute-start.12 = (f32[4,16,128]{2,1,0:T(8,128)S(1)}, f32[4,16,128]{2,1,0:T(8,128)S(1)}, u32[]{:S(2)}, u32[]{:S(2)}) collective-permute-start(f32[4,16,128]{2,1,0:T(8,128)S(1)} %bitcast.375), channel_id=1, source_target_pairs={{0,13},{1,12},{2,15},{3,14},{4,9},{5,8},{6,11},{7,10},{8,5},{9,4},... | collective-permute-start | bytes 98312 | tf_op jit(solution)/shard_map/ppermute | solution.py:26
  253.2 5.2 %collective-permute-start.14 = (f32[4,16,128]{2,1,0:T(8,128)S(1)}, f32[4,16,128]{2,1,0:T(8,128)S(1)}, u32[]{:S(2)}, u32[]{:S(2)}) collective-permute-start(f32[4,16,128]{2,1,0:T(8,128)S(1)} %bitcast.373), channel_id=1, source_target_pairs={{0,15},{1,14},{2,13},{3,12},{4,11},{5,10},{6,9},{7,8},{8,7},{9,6},... | collective-permute-start | bytes 98312 | tf_op jit(solution)/shard_map/ppermute | solution.py:26
  260.1 73.0 %while.68 = (s32[]{:T(128)}, f32[4,16,2048]{2,1,0:T(8,128)S(1)}, f32[4,16,2048]{2,1,0:T(8,128)S(1)}, s32[]{:T(128)}, s32[]{:T(128)}, /*index=5*/s32[]{:T(128)}, s32[]{:T(128)}) while((s32[]{:T(128)}, f32[4,16,2048]{2,1,0:T(8,128)S(1)}, f32[4,16,2048]{2,1,0:T(8,128)S(1)}, s32[]{:T(128)}, s32[]{:T(128)}, ...), condition=%wide.region_7.8_spmd.clone.clone, body=%wide.region_6.7_spmd.clone.clone.sunk | while | flops 410522368 | bytes 608387 | solution.py:74
  260.1 9.1 %fusion.166 = f32[4,16,2048]{2,1,0:T(8,128)S(1)} fusion(f32[4,16,2048]{2,1,0:T(8,128)S(1)} %get-tuple-element.886, s32[]{:T(128)S(6)} %select_n.305, f32[4,16,2048]{2,1,0:T(8,128)S(1)} %get-tuple-element.894, s32[256]{0:T(256)S(1)} %multiply_add_fusion.3, f32[2048]{0:T(1024)S(1)} %fusion.165), kind=kOutput, calls=%fused_computation.50.clone.1 | convolution fusion | flops 410517504 | bytes 599044 | tf_op jit(solution)/shard_map/while/body/eval_jaxpr/zyk,kx->zyx/dot_general | solution.py:71
  269.3 9.1 %fusion.166 = f32[4,16,2048]{2,1,0:T(8,128)S(1)} fusion(f32[4,16,2048]{2,1,0:T(8,128)S(1)} %get-tuple-element.886, s32[]{:T(128)S(6)} %select_n.305, f32[4,16,2048]{2,1,0:T(8,128)S(1)} %get-tuple-element.894, s32[256]{0:T(256)S(1)} %multiply_add_fusion.3, f32[2048]{0:T(1024)S(1)} %fusion.165), kind=kOutput, calls=%fused_computation.50.clone.1 | convolution fusion | flops 410517504 | bytes 599044 | tf_op jit(solution)/shard_map/while/body/eval_jaxpr/zyk,kx->zyx/dot_general | solution.py:71
  278.4 9.1 %fusion.166 = f32[4,16,2048]{2,1,0:T(8,128)S(1)} fusion(f32[4,16,2048]{2,1,0:T(8,128)S(1)} %get-tuple-element.886, s32[]{:T(128)S(6)} %select_n.305, f32[4,16,2048]{2,1,0:T(8,128)S(1)} %get-tuple-element.894, s32[256]{0:T(256)S(1)} %multiply_add_fusion.3, f32[2048]{0:T(1024)S(1)} %fusion.165), kind=kOutput, calls=%fused_computation.50.clone.1 | convolution fusion | flops 410517504 | bytes 599044 | tf_op jit(solution)/shard_map/while/body/eval_jaxpr/zyk,kx->zyx/dot_general | solution.py:71
  287.5 9.1 %fusion.166 = f32[4,16,2048]{2,1,0:T(8,128)S(1)} fusion(f32[4,16,2048]{2,1,0:T(8,128)S(1)} %get-tuple-element.886, s32[]{:T(128)S(6)} %select_n.305, f32[4,16,2048]{2,1,0:T(8,128)S(1)} %get-tuple-element.894, s32[256]{0:T(256)S(1)} %multiply_add_fusion.3, f32[2048]{0:T(1024)S(1)} %fusion.165), kind=kOutput, calls=%fused_computation.50.clone.1 | convolution fusion | flops 410517504 | bytes 599044 | tf_op jit(solution)/shard_map/while/body/eval_jaxpr/zyk,kx->zyx/dot_general | solution.py:71
  296.6 9.1 %fusion.166 = f32[4,16,2048]{2,1,0:T(8,128)S(1)} fusion(f32[4,16,2048]{2,1,0:T(8,128)S(1)} %get-tuple-element.886, s32[]{:T(128)S(6)} %select_n.305, f32[4,16,2048]{2,1,0:T(8,128)S(1)} %get-tuple-element.894, s32[256]{0:T(256)S(1)} %multiply_add_fusion.3, f32[2048]{0:T(1024)S(1)} %fusion.165), kind=kOutput, calls=%fused_computation.50.clone.1 | convolution fusion | flops 410517504 | bytes 599044 | tf_op jit(solution)/shard_map/while/body/eval_jaxpr/zyk,kx->zyx/dot_general | solution.py:71
  305.8 9.1 %fusion.166 = f32[4,16,2048]{2,1,0:T(8,128)S(1)} fusion(f32[4,16,2048]{2,1,0:T(8,128)S(1)} %get-tuple-element.886, s32[]{:T(128)S(6)} %select_n.305, f32[4,16,2048]{2,1,0:T(8,128)S(1)} %get-tuple-element.894, s32[256]{0:T(256)S(1)} %multiply_add_fusion.3, f32[2048]{0:T(1024)S(1)} %fusion.165), kind=kOutput, calls=%fused_computation.50.clone.1 | convolution fusion | flops 410517504 | bytes 599044 | tf_op jit(solution)/shard_map/while/body/eval_jaxpr/zyk,kx->zyx/dot_general | solution.py:71
  314.9 9.1 %fusion.166 = f32[4,16,2048]{2,1,0:T(8,128)S(1)} fusion(f32[4,16,2048]{2,1,0:T(8,128)S(1)} %get-tuple-element.886, s32[]{:T(128)S(6)} %select_n.305, f32[4,16,2048]{2,1,0:T(8,128)S(1)} %get-tuple-element.894, s32[256]{0:T(256)S(1)} %multiply_add_fusion.3, f32[2048]{0:T(1024)S(1)} %fusion.165), kind=kOutput, calls=%fused_computation.50.clone.1 | convolution fusion | flops 410517504 | bytes 599044 | tf_op jit(solution)/shard_map/while/body/eval_jaxpr/zyk,kx->zyx/dot_general | solution.py:71
  324.0 9.1 %fusion.166 = f32[4,16,2048]{2,1,0:T(8,128)S(1)} fusion(f32[4,16,2048]{2,1,0:T(8,128)S(1)} %get-tuple-element.886, s32[]{:T(128)S(6)} %select_n.305, f32[4,16,2048]{2,1,0:T(8,128)S(1)} %get-tuple-element.894, s32[256]{0:T(256)S(1)} %multiply_add_fusion.3, f32[2048]{0:T(1024)S(1)} %fusion.165), kind=kOutput, calls=%fused_computation.50.clone.1 | convolution fusion | flops 410517504 | bytes 599044 | tf_op jit(solution)/shard_map/while/body/eval_jaxpr/zyk,kx->zyx/dot_general | solution.py:71
  336.1 4.8 %reshape.130 = f32[32,1,4096]{2,1,0:T(1,128)S(1)} reshape(f32[2048,4,16]{2,1,0:T(4,128)} %bitcast.355) | data formatting | bytes 1048576
  340.9 21.0 %all_to_all.54 = f32[32,1,4096]{2,1,0:T(1,128)S(1)} all-to-all(f32[32,1,4096]{2,1,0:T(1,128)S(1)} %reshape.130), channel_id=1, replica_groups=mesh['gx'=32,'gy'=16] {'gx'}, dimensions={0} | all-to-all | bytes 1048576 | tf_op jit(solution)/shard_map/all_to_all | solution.py:121
  (867 shorter events, 91.9 us)
Async XLA Ops:
  0.0 1.0 copy-start
  3.9 30.0 %all-to-all-start = ((f32[32,1,4096]{2,1,0:T(1,128)}), f32[32,1,4096]{2,1,0:T(1,128)S(1)}, u32[]{:S(2)}, u32[]{:S(2)}) async-start(f32[32,1,4096]{2,1,0:T(1,128)} %reshape.126), calls=%async_computation | async-start | bytes 1048576 | tf_op jit(solution)/shard_map/all_to_all | solution.py:109
  123.8 38.3 %all-to-all-start.1 = ((f32[16,1,8192]{2,1,0:T(1,128)}), f32[16,1,8192]{2,1,0:T(1,128)S(1)}, u32[]{:S(2)}, u32[]{:S(2)}) async-start(f32[16,1,8192]{2,1,0:T(1,128)} %reshape.128), calls=%async_computation.1 | async-start | bytes 1048576 | tf_op jit(solution)/shard_map/all_to_all | solution.py:113
  203.7 14.2 %collective-permute-start = (f32[4,16,128]{2,1,0:T(8,128)S(1)}, f32[4,16,128]{2,1,0:T(8,128)S(1)}, u32[]{:S(2)}, u32[]{:S(2)}) collective-permute-start(f32[4,16,128]{2,1,0:T(8,128)S(1)} %bitcast.387), channel_id=1, source_target_pairs={{0,1},{1,0},{2,3},{3,2},{4,5},{5,4},{6,7},{7,6},{8,9},{9,8},{10,11... | collective-permute-start | bytes 98312 | tf_op jit(solution)/shard_map/ppermute | solution.py:26
  205.6 15.5 %collective-permute-start.1 = (f32[4,16,128]{2,1,0:T(8,128)S(1)}, f32[4,16,128]{2,1,0:T(8,128)S(1)}, u32[]{:S(2)}, u32[]{:S(2)}) collective-permute-start(f32[4,16,128]{2,1,0:T(8,128)S(1)} %bitcast.386), channel_id=1, source_target_pairs={{0,2},{1,3},{2,0},{3,1},{4,6},{5,7},{6,4},{7,5},{8,10},{9,11},{10,... | collective-permute-start | bytes 98312 | tf_op jit(solution)/shard_map/ppermute | solution.py:26
  207.6 18.2 %collective-permute-start.2 = (f32[4,16,128]{2,1,0:T(8,128)S(1)}, f32[4,16,128]{2,1,0:T(8,128)S(1)}, u32[]{:S(2)}, u32[]{:S(2)}) collective-permute-start(f32[4,16,128]{2,1,0:T(8,128)S(1)} %bitcast.385), channel_id=1, source_target_pairs={{0,3},{1,2},{2,1},{3,0},{4,7},{5,6},{6,5},{7,4},{8,11},{9,10},{10,... | collective-permute-start | bytes 98312 | tf_op jit(solution)/shard_map/ppermute | solution.py:26
  211.6 17.0 %collective-permute-start.3 = (f32[4,16,128]{2,1,0:T(8,128)S(1)}, f32[4,16,128]{2,1,0:T(8,128)S(1)}, u32[]{:S(2)}, u32[]{:S(2)}) collective-permute-start(f32[4,16,128]{2,1,0:T(8,128)S(1)} %bitcast.384), channel_id=1, source_target_pairs={{0,4},{1,5},{2,6},{3,7},{4,0},{5,1},{6,2},{7,3},{8,12},{9,13},{10,... | collective-permute-start | bytes 98312 | tf_op jit(solution)/shard_map/ppermute | solution.py:26
  213.6 21.3 %collective-permute-start.4 = (f32[4,16,128]{2,1,0:T(8,128)S(1)}, f32[4,16,128]{2,1,0:T(8,128)S(1)}, u32[]{:S(2)}, u32[]{:S(2)}) collective-permute-start(f32[4,16,128]{2,1,0:T(8,128)S(1)} %bitcast.383), channel_id=1, source_target_pairs={{0,5},{1,4},{2,7},{3,6},{4,1},{5,0},{6,3},{7,2},{8,13},{9,12},{10,... | collective-permute-start | bytes 98312 | tf_op jit(solution)/shard_map/ppermute | solution.py:26
  217.9 18.9 %collective-permute-start.5 = (f32[4,16,128]{2,1,0:T(8,128)S(1)}, f32[4,16,128]{2,1,0:T(8,128)S(1)}, u32[]{:S(2)}, u32[]{:S(2)}) collective-permute-start(f32[4,16,128]{2,1,0:T(8,128)S(1)} %bitcast.382), channel_id=1, source_target_pairs={{0,6},{1,7},{2,4},{3,5},{4,2},{5,3},{6,0},{7,1},{8,14},{9,15},{10,... | collective-permute-start | bytes 98312 | tf_op jit(solution)/shard_map/ppermute | solution.py:26
  221.1 22.8 %collective-permute-start.6 = (f32[4,16,128]{2,1,0:T(8,128)S(1)}, f32[4,16,128]{2,1,0:T(8,128)S(1)}, u32[]{:S(2)}, u32[]{:S(2)}) collective-permute-start(f32[4,16,128]{2,1,0:T(8,128)S(1)} %bitcast.381), channel_id=1, source_target_pairs={{0,7},{1,6},{2,5},{3,4},{4,3},{5,2},{6,1},{7,0},{8,15},{9,14},{10,... | collective-permute-start | bytes 98312 | tf_op jit(solution)/shard_map/ppermute | solution.py:26
  225.7 20.1 %collective-permute-start.7 = (f32[4,16,128]{2,1,0:T(8,128)S(1)}, f32[4,16,128]{2,1,0:T(8,128)S(1)}, u32[]{:S(2)}, u32[]{:S(2)}) collective-permute-start(f32[4,16,128]{2,1,0:T(8,128)S(1)} %bitcast.380), channel_id=1, source_target_pairs={{0,8},{1,9},{2,10},{3,11},{4,12},{5,13},{6,14},{7,15},{8,0},{9,1},... | collective-permute-start | bytes 98312 | tf_op jit(solution)/shard_map/ppermute | solution.py:26
  228.7 22.6 %collective-permute-start.8 = (f32[4,16,128]{2,1,0:T(8,128)S(1)}, f32[4,16,128]{2,1,0:T(8,128)S(1)}, u32[]{:S(2)}, u32[]{:S(2)}) collective-permute-start(f32[4,16,128]{2,1,0:T(8,128)S(1)} %bitcast.379), channel_id=1, source_target_pairs={{0,9},{1,8},{2,11},{3,10},{4,13},{5,12},{6,15},{7,14},{8,1},{9,0},... | collective-permute-start | bytes 98312 | tf_op jit(solution)/shard_map/ppermute | solution.py:26
  234.9 18.3 %collective-permute-start.9 = (f32[4,16,128]{2,1,0:T(8,128)S(1)}, f32[4,16,128]{2,1,0:T(8,128)S(1)}, u32[]{:S(2)}, u32[]{:S(2)}) collective-permute-start(f32[4,16,128]{2,1,0:T(8,128)S(1)} %bitcast.378), channel_id=1, source_target_pairs={{0,10},{1,11},{2,8},{3,9},{4,14},{5,15},{6,12},{7,13},{8,2},{9,3},... | collective-permute-start | bytes 98312 | tf_op jit(solution)/shard_map/ppermute | solution.py:26
  236.8 21.7 %collective-permute-start.10 = (f32[4,16,128]{2,1,0:T(8,128)S(1)}, f32[4,16,128]{2,1,0:T(8,128)S(1)}, u32[]{:S(2)}, u32[]{:S(2)}) collective-permute-start(f32[4,16,128]{2,1,0:T(8,128)S(1)} %bitcast.377), channel_id=1, source_target_pairs={{0,11},{1,10},{2,9},{3,8},{4,15},{5,14},{6,13},{7,12},{8,3},{9,2},... | collective-permute-start | bytes 98312 | tf_op jit(solution)/shard_map/ppermute | solution.py:26
  243.9 14.6 %collective-permute-start.11 = (f32[4,16,128]{2,1,0:T(8,128)S(1)}, f32[4,16,128]{2,1,0:T(8,128)S(1)}, u32[]{:S(2)}, u32[]{:S(2)}) collective-permute-start(f32[4,16,128]{2,1,0:T(8,128)S(1)} %bitcast.376), channel_id=1, source_target_pairs={{0,12},{1,13},{2,14},{3,15},{4,8},{5,9},{6,10},{7,11},{8,4},{9,5},... | collective-permute-start | bytes 98312 | tf_op jit(solution)/shard_map/ppermute | solution.py:26
  245.9 12.7 %collective-permute-start.12 = (f32[4,16,128]{2,1,0:T(8,128)S(1)}, f32[4,16,128]{2,1,0:T(8,128)S(1)}, u32[]{:S(2)}, u32[]{:S(2)}) collective-permute-start(f32[4,16,128]{2,1,0:T(8,128)S(1)} %bitcast.375), channel_id=1, source_target_pairs={{0,13},{1,12},{2,15},{3,14},{4,9},{5,8},{6,11},{7,10},{8,5},{9,4},... | collective-permute-start | bytes 98312 | tf_op jit(solution)/shard_map/ppermute | solution.py:26
  251.3 7.3 %collective-permute-start.13 = (f32[4,16,128]{2,1,0:T(8,128)S(1)}, f32[4,16,128]{2,1,0:T(8,128)S(1)}, u32[]{:S(2)}, u32[]{:S(2)}) collective-permute-start(f32[4,16,128]{2,1,0:T(8,128)S(1)} %bitcast.374), channel_id=1, source_target_pairs={{0,14},{1,15},{2,12},{3,13},{4,10},{5,11},{6,8},{7,9},{8,6},{9,7},... | collective-permute-start | bytes 98312 | tf_op jit(solution)/shard_map/ppermute | solution.py:26
  253.2 6.8 %collective-permute-start.14 = (f32[4,16,128]{2,1,0:T(8,128)S(1)}, f32[4,16,128]{2,1,0:T(8,128)S(1)}, u32[]{:S(2)}, u32[]{:S(2)}) collective-permute-start(f32[4,16,128]{2,1,0:T(8,128)S(1)} %bitcast.373), channel_id=1, source_target_pairs={{0,15},{1,14},{2,13},{3,12},{4,11},{5,10},{6,9},{7,8},{8,7},{9,6},... | collective-permute-start | bytes 98312 | tf_op jit(solution)/shard_map/ppermute | solution.py:26
